TPU v7x, 128 devices: a whole 4x4x4 slice. The times are simulated.
128 devices in a mesh: col: 32 (over z, y, x_hi), row: 4 (over x_lo, core).
Axes of the slice: x: 4 (x_hi: 2, x_lo: 2; x = x_hi * 2 + x_lo), y: 4, z: 4, core: 2. Of those that a mesh axis runs over, the one named last changes fastest.
Arguments:
- hamiltonian: float32 [16384, 16384], P('row', 'col'), as said below
Outputs:
- reduced: float32 [16384, 16384], P('row', 'col')
Inputs may be any that keep to these rules, and one draw needn't show every extreme that they name: hamiltonian is symmetric.
All inputs are finite; a program needn't handle non-finite values.
Results may differ from a plain program's by a relative error of at most 0.00019.
Values sent between devices are 32-bit elements; how exact they have to be, the bound alone decides.
No kernel may reach another device: no remote copies, remote signals or barrier semaphores. Data moves between devices by JAX's collectives and lax.ppermute only.
A program may use at most 128 MiB of HBM per device.

v0:
```python
import jax
import jax.numpy as jnp
from jax import lax
from jax.sharding import PartitionSpec as P

NB = 256
PANELS = 2


def from_root(block, axis, holder):
    block = jnp.where(lax.axis_index(axis) == holder, block, jnp.zeros_like(block))
    return lax.psum(block, axis)


def product(left, right):
    return jnp.dot(left, right, precision=lax.Precision.HIGHEST, preferred_element_type=jnp.float32)


def inner_tn(left, right):
    return lax.dot_general(
        left,
        right,
        (((0,), (0,)), ((), ())),
        precision=lax.Precision.HIGHEST,
        preferred_element_type=jnp.float32,
    )


def outer_nt(left, right):
    return lax.dot_general(
        left,
        right,
        (((1,), (1,)), ((), ())),
        precision=lax.Precision.HIGHEST,
        preferred_element_type=jnp.float32,
    )


def solve_right(gram, panel):
    lower = jnp.linalg.cholesky(gram)
    return lax.linalg.triangular_solve(lower, panel, left_side=False, lower=True, transpose_a=True)


def coupling_of(top_rows):
    square = jnp.eye(NB, dtype=jnp.float32) - top_rows.T
    normal_eq = inner_tn(square, square)
    factor = jnp.linalg.cholesky(normal_eq)
    middle = lax.linalg.triangular_solve(factor, square.T, left_side=True, lower=True)
    return lax.linalg.triangular_solve(factor, middle, left_side=True, lower=True, transpose_a=True)


def shards(hamiltonian):
    matrix = hamiltonian
    row_block = matrix.shape[0]
    col_block = matrix.shape[1]
    ratio = lax.axis_size("col") // lax.axis_size("row")
    row_pos = lax.axis_index("row")
    col_pos = lax.axis_index("col")
    global_rows = row_pos * row_block + jnp.arange(row_block, dtype=jnp.int32)
    owner = col_pos // ratio
    offset = col_pos % ratio * col_block
    for panel_index in range(PANELS):
        first_col = panel_index * NB
        first_row = first_col + NB
        live = (global_rows >= first_row)[:, None]
        panel = jnp.where(live, matrix[:, first_col : first_col + NB], jnp.float32(0.0))
        gram = lax.psum(inner_tn(panel, panel), "row")
        basis = solve_right(gram, panel)
        top_rows = from_root(basis[first_row : first_row + NB], "row", 0)
        coupling = coupling_of(top_rows)
        ident = (
            global_rows[:, None] - first_row == jnp.arange(NB, dtype=jnp.int32)[None, :]
        ).astype(jnp.float32)
        vectors = ident - basis
        vectors, coupling = (from_root(vectors, "col", 0), from_root(coupling, "col", 0))
        column_vectors = from_root(
            lax.dynamic_slice_in_dim(vectors, offset, col_block, 0), "row", owner
        )
        applied = lax.psum(product(matrix, column_vectors), "col")
        applied = product(applied, coupling)
        inner = lax.psum(inner_tn(vectors, applied), "row")
        inner = product(coupling.T, inner)
        shifted = applied - 0.5 * product(vectors, inner)
        column_shifted = from_root(
            lax.dynamic_slice_in_dim(shifted, offset, col_block, 0), "row", owner
        )
        matrix = matrix - outer_nt(vectors, column_shifted) - outer_nt(shifted, column_vectors)
    return matrix


def solution(mesh):
    return jax.shard_map(
        shards, mesh=mesh, in_specs=(P("row", "col"),), out_specs=P("row", "col"), check_vma=False
    )
```

profile of v0, /device:TPU:1, one launch (start us, length us, event | category | flops | bytes accessed | tf_op | source)
XLA Modules:
  0.0 2289.1 jit_solution(8985189598274994049)
XLA Ops:
  24.4 39.6 %all-reduce.18.cloned.1.call-done = f32[256,256]{0,1:T(8,128)} async-done(((f32[256,256]{0,1:T(8,128)}), f32[256,256]{0,1:T(8,128)}) %all-reduce.18.cloned.1.call-update) | async-done | bytes 262160 | tf_op jit(solution)/shard_map/psum | solution.py:67
  66.1 11.7 cholesky.214
  77.8 9.8 custom-call.23
  88.2 11.7 cholesky.231
  106.4 19.7 custom-call.24
  139.4 357.7 %all-reduce.20.cloned.1.call-done = f32[4096,256]{0,1:T(8,128)} async-done(((f32[4096,256]{0,1:T(8,128)}), f32[4096,256]{0,1:T(8,128)}) %all-reduce.20.cloned.1.call-update) | async-done | bytes 4194320 | tf_op jit(solution)/shard_map/psum | solution.py:12
  499.5 60.5 %all-reduce.40.cloned.1.call-done = (f32[512,256]{0,1:T(8,128)}, f32[256,256]{0,1:T(8,128)}) async-done(((f32[512,256]{0,1:T(8,128)}, f32[256,256]{0,1:T(8,128)}), (f32[512,256]{0,1:T(8,128)}, f32[256,256]{0,1:T(8,128)})) %all-reduce.40.cloned.1.call-update) | async-done | bytes 786448 | tf_op jit(solution)/shard_map/psum | solution.py:12
  562.9 11.7 cholesky.248
  574.7 9.8 custom-call.25
  585.0 11.7 cholesky.265
  603.5 19.7 custom-call.27
  625.4 10.9 convolution_bitcast_fusion
  637.0 362.5 %all-reduce.36.cloned.1.call-done = (f32[4096,256]{0,1:T(8,128)}, f32[256,256]{0,1:T(8,128)}) async-done(((f32[4096,256]{0,1:T(8,128)}, f32[256,256]{0,1:T(8,128)}), (f32[4096,256]{0,1:T(8,128)}, f32[256,256]{0,1:T(8,128)})) %all-reduce.36.cloned.1.call-update) | async-done | bytes 4456464 | tf_op jit(solution)/shard_map/psum | solution.py:79
  1020.5 50.7 %all-reduce.22.cloned.1.call-done = f32[256,256]{1,0:T(8,128)} async-done(((f32[256,256]{1,0:T(8,128)}), f32[256,256]{1,0:T(8,128)}) %all-reduce.22.cloned.1.call-update) | async-done | bytes 262160 | tf_op jit(solution)/shard_map/psum | solution.py:81
  1083.5 38.6 %all-reduce.24.cloned.1.call-done = f32[512,256]{0,1:T(8,128)} async-done(((f32[512,256]{0,1:T(8,128)}), f32[512,256]{0,1:T(8,128)}) %all-reduce.24.cloned.1.call-update) | async-done | bytes 524304 | tf_op jit(solution)/shard_map/psum | solution.py:12
  1122.2 10.1 fusion.64
  1132.2 11.0 subtract_subtract_fusion.1
  1153.1 36.9 %all-reduce.26.cloned.1.call-done = f32[256,256]{0,1:T(8,128)} async-done(((f32[256,256]{0,1:T(8,128)}), f32[256,256]{0,1:T(8,128)}) %all-reduce.26.cloned.1.call-update) | async-done | bytes 262160 | tf_op jit(solution)/shard_map/psum | solution.py:67
  1192.1 11.7 cholesky.282
  1203.8 9.8 custom-call.28
  1214.1 11.7 cholesky.299
  1232.9 19.7 custom-call.29
  1265.9 357.7 %all-reduce.28.cloned.1.call-done = f32[4096,256]{0,1:T(8,128)} async-done(((f32[4096,256]{0,1:T(8,128)}), f32[4096,256]{0,1:T(8,128)}) %all-reduce.28.cloned.1.call-update) | async-done | bytes 4194320 | tf_op jit(solution)/shard_map/psum | solution.py:12
  1626.1 60.3 %all-reduce.38.cloned.1.call-done = (f32[512,256]{0,1:T(8,128)}, f32[256,256]{0,1:T(8,128)}) async-done(((f32[512,256]{0,1:T(8,128)}, f32[256,256]{0,1:T(8,128)}), (f32[512,256]{0,1:T(8,128)}, f32[256,256]{0,1:T(8,128)})) %all-reduce.38.cloned.1.call-update) | async-done | bytes 786448 | tf_op jit(solution)/shard_map/psum | solution.py:12
  1689.2 11.7 cholesky.316
  1711.3 11.7 cholesky.333
  1730.2 19.7 custom-call.32
  1752.0 16.9 fusion.66
  1769.7 362.3 %all-reduce.34.cloned.1.call-done = (f32[4096,256]{1,0:T(8,128)}, f32[256,256]{0,1:T(8,128)}) async-done(((f32[4096,256]{1,0:T(8,128)}, f32[256,256]{0,1:T(8,128)}), (f32[4096,256]{1,0:T(8,128)}, f32[256,256]{0,1:T(8,128)})) %all-reduce.34.cloned.1.call-update) | async-done | bytes 4456464 | tf_op jit(solution)/shard_map/psum | solution.py:79
  2149.8 50.4 %all-reduce.30.cloned.1.call-done = f32[256,256]{1,0:T(8,128)} async-done(((f32[256,256]{1,0:T(8,128)}), f32[256,256]{1,0:T(8,128)}) %all-reduce.30.cloned.1.call-update) | async-done | bytes 262160 | tf_op jit(solution)/shard_map/psum | solution.py:81
  2212.4 38.7 %all-reduce.32.cloned.1.call-done = f32[512,256]{0,1:T(8,128)} async-done(((f32[512,256]{0,1:T(8,128)}), f32[512,256]{0,1:T(8,128)}) %all-reduce.32.cloned.1.call-update) | async-done | bytes 524304 | tf_op jit(solution)/shard_map/psum | solution.py:12
  2260.7 12.4 subtract_subtract_fusion
  (195 shorter events, 206.3 us)
Async XLA Ops:
  6.5 57.5 %all-reduce.18.cloned.1.call-start = ((), (), s32[]{:S(2)}) async-start(), calls=%async_computation | async-start | bytes 524288 | tf_op jit(solution)/shard_map/psum | solution.py:67
  18.0 1.9 copy-start.1
  24.1 473.0 %all-reduce.20.cloned.1.call-start = ((), (), s32[]{:S(2)}) async-start(), calls=%async_computation.1 | async-start | bytes 8388608 | tf_op jit(solution)/shard_map/psum | solution.py:12
  126.0 3.7 copy-start.2
  133.7 1.4 copy-start.13
  137.6 422.4 %all-reduce.40.cloned.1.call-start = ((), (), s32[]{:S(2)}) async-start(), calls=%async_computation.11 | async-start | bytes 1572864 | tf_op jit(solution)/shard_map/psum | solution.py:12
  499.1 500.5 %all-reduce.36.cloned.1.call-start = ((), (), s32[]{:S(2)}) async-start(), calls=%async_computation.9 | async-start | bytes 8912896 | tf_op jit(solution)/shard_map/psum | solution.py:79
  560.0 65.3 %copy-start.16 = (f32[512,256]{0,1:T(8,128)S(1)}, f32[512,256]{0,1:T(8,128)}, u32[]{:S(2)}) copy-start(f32[512,256]{0,1:T(8,128)} %get-tuple-element.95) | copy-start | bytes 1572868
  637.0 434.2 %all-reduce.22.cloned.1.call-start = ((), (), s32[]{:S(2)}) async-start(), calls=%async_computation.2 | async-start | bytes 524288 | tf_op jit(solution)/shard_map/psum | solution.py:81
  999.5 10.8 copy-start.5
  1008.4 2.0 copy-start.7
  1014.7 56.5 %copy-start.17 = (f32[256,256]{0,1:T(8,128)S(1)}, f32[256,256]{0,1:T(8,128)}, u32[]{:S(2)}) copy-start(f32[256,256]{0,1:T(8,128)} %get-tuple-element.92) | copy-start | bytes 786436
  1014.7 107.5 %all-reduce.24.cloned.1.call-start = ((), (), s32[]{:S(2)}) async-start(), calls=%async_computation.3 | async-start | bytes 1048576 | tf_op jit(solution)/shard_map/psum | solution.py:12
  1080.6 2.0 copy-start.9
  1083.5 106.5 %all-reduce.26.cloned.1.call-start = ((), (), s32[]{:S(2)}) async-start(), calls=%async_computation.4 | async-start | bytes 524288 | tf_op jit(solution)/shard_map/psum | solution.py:67
  1122.2 10.1 copy-start.10
  1143.3 3.4 copy-start
  1146.7 1.9 copy-start.3
  1152.9 470.8 %all-reduce.28.cloned.1.call-start = ((), (), s32[]{:S(2)}) async-start(), calls=%async_computation.5 | async-start | bytes 8388608 | tf_op jit(solution)/shard_map/psum | solution.py:12
  1252.6 3.7 copy-start.4
  1260.3 1.4 copy-start.14
  1264.2 422.2 %all-reduce.38.cloned.1.call-start = ((), (), s32[]{:S(2)}) async-start(), calls=%async_computation.10 | async-start | bytes 1572864 | tf_op jit(solution)/shard_map/psum | solution.py:12
  1625.6 506.5 %all-reduce.34.cloned.1.call-start = ((), (), s32[]{:S(2)}) async-start(), calls=%async_computation.8 | async-start | bytes 8912896 | tf_op jit(solution)/shard_map/psum | solution.py:79
  1686.4 65.6 %copy-start.15 = (f32[512,256]{0,1:T(8,128)S(1)}, f32[512,256]{0,1:T(8,128)}, u32[]{:S(2)}) copy-start(f32[512,256]{0,1:T(8,128)} %get-tuple-element.93) | copy-start | bytes 1572868
  1769.6 430.5 %all-reduce.30.cloned.1.call-start = ((), (), s32[]{:S(2)}) async-start(), calls=%async_computation.6 | async-start | bytes 524288 | tf_op jit(solution)/shard_map/psum | solution.py:81
  2132.0 7.4 copy-start.6
  2137.5 2.0 copy-start.8
  2143.8 56.3 %copy-start.18 = (f32[256,256]{0,1:T(8,128)S(1)}, f32[256,256]{0,1:T(8,128)}, u32[]{:S(2)}) copy-start(f32[256,256]{0,1:T(8,128)} %get-tuple-element.90) | copy-start | bytes 786436
  2143.8 107.3 %all-reduce.32.cloned.1.call-start = ((), (), s32[]{:S(2)}) async-start(), calls=%async_computation.7 | async-start | bytes 1048576 | tf_op jit(solution)/shard_map/psum | solution.py:12
  2209.5 2.0 copy-start.11
  2251.1 9.6 copy-start.12
Sparse Core Ops, SparseCore 0:
  24.3 39.6 all-reduce.17
  137.8 359.3 all-reduce.19
  499.9 60.0 all-reduce.39
  637.1 362.3 all-reduce.35
  1014.8 56.3 all-reduce.21
  1083.6 38.5 all-reduce.23
  1153.0 36.9 all-reduce.25
  1264.3 359.2 all-reduce.27
  1626.2 60.0 all-reduce.37
  1769.8 362.2 all-reduce.33
  2143.9 56.1 all-reduce.29
  2212.5 38.5 all-reduce.31
where the time goes:
time: 2290 us
  waiting for transfers between devices  1820 us (79%)
  other arithmetic  239 us (10%)
  matrix products  145 us (6%)
  local copies, waits for them, and re-layouts  65.9 us (3%)
    psum x6, waiting for transfers between devices, from_root(): return lax.psum(block, axis)  914 us
    psum x2, waiting for transfers between devices, shards(): applied = lax.psum(product(matrix, column_vectors), 'col')  725 us
    psum x2, waiting for transfers between devices, shards(): inner = lax.psum(inner_tn(vectors, applied), 'row')  101 us
    psum x2, waiting for transfers between devices, shards(): gram = lax.psum(inner_tn(panel, panel), 'row')  76.5 us
    another operation x14, other arithmetic, coupling_of(): factor = jnp.linalg.cholesky(normal_eq)  69.4 us
    another operation x13, other arithmetic, solve_right(): lower = jnp.linalg.cholesky(gram)  68.7 us
    dot_general x8, matrix products, product(): jnp.dot(left, right, precision=lax.Precision.HIGHEST, preferred_element_t...  60.7 us
  transfers between devices with their start and end apart: 12, of which 12 were waited for; matrix products, arithmetic and copies ran while one was open for 1% of the time, Pallas kernels for 0%

commit v1 on v0

--- a/solution.py
+++ b/solution.py
@@ -78,7 +78,7 @@
         )
         applied = lax.psum(product(matrix, column_vectors), "col")
         applied = product(applied, coupling)
-        inner = lax.psum(inner_tn(vectors, applied), "row")
+        inner = jnp.sum(lax.all_gather(inner_tn(vectors, applied), "row"), axis=0)
         inner = product(coupling.T, inner)
         shifted = applied - 0.5 * product(vectors, inner)
         column_shifted = from_root(

time: 2290 us -> 2260 us (0.987)
  waiting for transfers between devices: 1820 us -> 1790 us
    psum x2 -> x0, waiting for transfers between devices: 101 us -> none  [shards(): inner = lax.psum(inner_tn(vectors, applied), 'row')]
    all_gather x0 -> x2, waiting for transfers between devices: none -> 70.1 us  [shards(): inner = jnp.sum(lax.all_gather(inner_tn(vectors, applied), 'row'), axis=0)]
where the time goes in v1:
time: 2260 us
  waiting for transfers between devices  1790 us (79%)
  other arithmetic  242 us (11%)
  matrix products  143 us (6%)
  local copies, waits for them, and re-layouts  65.9 us (3%)
    psum x6, waiting for transfers between devices, from_root(): return lax.psum(block, axis)  914 us
    psum x2, waiting for transfers between devices, shards(): applied = lax.psum(product(matrix, column_vectors), 'col')  725 us
    psum x2, waiting for transfers between devices, shards(): gram = lax.psum(inner_tn(panel, panel), 'row')  76.5 us
    all_gather x2, waiting for transfers between devices, shards(): inner = jnp.sum(lax.all_gather(inner_tn(vectors, applied), 'row'), axis=0)  70.1 us
    another operation x14, other arithmetic, coupling_of(): factor = jnp.linalg.cholesky(normal_eq)  69.4 us
    another operation x13, other arithmetic, solve_right(): lower = jnp.linalg.cholesky(gram)  68.7 us
    dot_general x8, matrix products, product(): jnp.dot(left, right, precision=lax.Precision.HIGHEST, preferred_element_t...  58.9 us
  transfers between devices with their start and end apart: 12, of which 12 were waited for; matrix products, arithmetic and copies ran while one was open for 1% of the time, Pallas kernels for 0%

profile of v1, /device:TPU:1, one launch (start us, length us, event | category | flops | bytes accessed | tf_op | source)
XLA Modules:
  0.0 2259.3 jit_solution(15180738569823051124)
XLA Ops:
  24.4 39.6 %all-reduce.16.cloned.1.call-done = f32[256,256]{0,1:T(8,128)} async-done(((f32[256,256]{0,1:T(8,128)}), f32[256,256]{0,1:T(8,128)}) %all-reduce.16.cloned.1.call-update) | async-done | bytes 262160 | tf_op jit(solution)/shard_map/psum | solution.py:67
  66.1 11.7 cholesky.214
  77.8 9.8 custom-call.23
  88.2 11.7 cholesky.231
  106.4 19.7 custom-call.24
  139.4 357.7 %all-reduce.18.cloned.1.call-done = f32[4096,256]{0,1:T(8,128)} async-done(((f32[4096,256]{0,1:T(8,128)}), f32[4096,256]{0,1:T(8,128)}) %all-reduce.18.cloned.1.call-update) | async-done | bytes 4194320 | tf_op jit(solution)/shard_map/psum | solution.py:12
  499.5 60.5 %all-reduce.34.cloned.1.call-done = (f32[512,256]{0,1:T(8,128)}, f32[256,256]{0,1:T(8,128)}) async-done(((f32[512,256]{0,1:T(8,128)}, f32[256,256]{0,1:T(8,128)}), (f32[512,256]{0,1:T(8,128)}, f32[256,256]{0,1:T(8,128)})) %all-reduce.34.cloned.1.call-update) | async-done | bytes 786448 | tf_op jit(solution)/shard_map/psum | solution.py:12
  562.9 11.7 cholesky.248
  574.7 9.8 custom-call.25
  585.0 11.7 cholesky.265
  603.5 19.7 custom-call.27
  625.4 10.9 convolution_bitcast_fusion
  637.0 362.5 %all-reduce.30.cloned.1.call-done = (f32[4096,256]{0,1:T(8,128)}, f32[256,256]{0,1:T(8,128)}) async-done(((f32[4096,256]{0,1:T(8,128)}, f32[256,256]{0,1:T(8,128)}), (f32[4096,256]{0,1:T(8,128)}, f32[256,256]{0,1:T(8,128)})) %all-reduce.30.cloned.1.call-update) | async-done | bytes 4456464 | tf_op jit(solution)/shard_map/psum | solution.py:79
  1020.4 35.1 %all-gather.5.cloned.1.call-done = f32[1024,256]{1,0:T(8,128)} async-done(((f32[256,256]{1,0:T(8,128)}), f32[1024,256]{1,0:T(8,128)}) %all-gather.5.cloned.1.call-update) | async-done | bytes 1048592 | tf_op jit(solution)/shard_map/all_gather | solution.py:81
  1068.3 38.6 %all-reduce.20.cloned.1.call-done = f32[512,256]{0,1:T(8,128)} async-done(((f32[512,256]{0,1:T(8,128)}), f32[512,256]{0,1:T(8,128)}) %all-reduce.20.cloned.1.call-update) | async-done | bytes 524304 | tf_op jit(solution)/shard_map/psum | solution.py:12
  1106.9 10.1 fusion.64
  1117.0 11.0 subtract_subtract_fusion.1
  1137.8 36.9 %all-reduce.22.cloned.1.call-done = f32[256,256]{0,1:T(8,128)} async-done(((f32[256,256]{0,1:T(8,128)}), f32[256,256]{0,1:T(8,128)}) %all-reduce.22.cloned.1.call-update) | async-done | bytes 262160 | tf_op jit(solution)/shard_map/psum | solution.py:67
  1176.8 11.7 cholesky.282
  1188.5 9.8 custom-call.28
  1198.8 11.7 cholesky.299
  1217.6 19.7 custom-call.29
  1250.6 357.8 %all-reduce.24.cloned.1.call-done = f32[4096,256]{0,1:T(8,128)} async-done(((f32[4096,256]{0,1:T(8,128)}), f32[4096,256]{0,1:T(8,128)}) %all-reduce.24.cloned.1.call-update) | async-done | bytes 4194320 | tf_op jit(solution)/shard_map/psum | solution.py:12
  1610.9 60.5 %all-reduce.32.cloned.1.call-done = (f32[512,256]{0,1:T(8,128)}, f32[256,256]{0,1:T(8,128)}) async-done(((f32[512,256]{0,1:T(8,128)}, f32[256,256]{0,1:T(8,128)}), (f32[512,256]{0,1:T(8,128)}, f32[256,256]{0,1:T(8,128)})) %all-reduce.32.cloned.1.call-update) | async-done | bytes 786448 | tf_op jit(solution)/shard_map/psum | solution.py:12
  1674.3 11.7 cholesky.316
  1696.3 11.7 cholesky.333
  1715.2 19.7 custom-call.32
  1737.0 16.9 fusion.66
  1754.7 362.6 %all-reduce.28.cloned.1.call-done = (f32[4096,256]{1,0:T(8,128)}, f32[256,256]{0,1:T(8,128)}) async-done(((f32[4096,256]{1,0:T(8,128)}, f32[256,256]{0,1:T(8,128)}), (f32[4096,256]{1,0:T(8,128)}, f32[256,256]{0,1:T(8,128)})) %all-reduce.28.cloned.1.call-update) | async-done | bytes 4456464 | tf_op jit(solution)/shard_map/psum | solution.py:79
  2135.0 34.9 %all-gather.7.cloned.1.call-done = f32[1024,256]{1,0:T(8,128)} async-done(((f32[256,256]{1,0:T(8,128)}), f32[1024,256]{1,0:T(8,128)}) %all-gather.7.cloned.1.call-update) | async-done | bytes 1048592 | tf_op jit(solution)/shard_map/all_gather | solution.py:81
  2182.6 38.6 %all-reduce.26.cloned.1.call-done = f32[512,256]{0,1:T(8,128)} async-done(((f32[512,256]{0,1:T(8,128)}), f32[512,256]{0,1:T(8,128)}) %all-reduce.26.cloned.1.call-update) | async-done | bytes 524304 | tf_op jit(solution)/shard_map/psum | solution.py:12
  2230.9 12.4 subtract_subtract_fusion
  (197 shorter events, 207.0 us)
Async XLA Ops:
  6.5 57.5 %all-reduce.16.cloned.1.call-start = ((), (), s32[]{:S(2)}) async-start(), calls=%async_computation | async-start | bytes 524288 | tf_op jit(solution)/shard_map/psum | solution.py:67
  18.0 1.9 copy-start.1
  24.1 473.0 %all-reduce.18.cloned.1.call-start = ((), (), s32[]{:S(2)}) async-start(), calls=%async_computation.1 | async-start | bytes 8388608 | tf_op jit(solution)/shard_map/psum | solution.py:12
  126.0 3.7 copy-start.2
  133.7 1.4 copy-start.13
  137.6 422.4 %all-reduce.34.cloned.1.call-start = ((), (), s32[]{:S(2)}) async-start(), calls=%async_computation.11 | async-start | bytes 1572864 | tf_op jit(solution)/shard_map/psum | solution.py:12
  499.1 500.4 %all-reduce.30.cloned.1.call-start = ((), (), s32[]{:S(2)}) async-start(), calls=%async_computation.9 | async-start | bytes 8912896 | tf_op jit(solution)/shard_map/psum | solution.py:79
  560.0 65.3 %copy-start.16 = (f32[512,256]{0,1:T(8,128)S(1)}, f32[512,256]{0,1:T(8,128)}, u32[]{:S(2)}) copy-start(f32[512,256]{0,1:T(8,128)} %get-tuple-element.95) | copy-start | bytes 1572868
  637.0 418.6 %all-gather.5.cloned.1.call-start = ((), (), s32[]{:S(2)}) async-start(), calls=%async_computation.6 | async-start | bytes 1310720 | tf_op jit(solution)/shard_map/all_gather | solution.py:81
  999.5 10.8 copy-start.5
  1008.4 2.0 copy-start.7
  1014.7 42.2 %copy-start.18 = (f32[256,256]{0,1:T(8,128)S(1)}, f32[256,256]{0,1:T(8,128)}, u32[]{:S(2)}) copy-start(f32[256,256]{0,1:T(8,128)} %get-tuple-element.92) | copy-start | bytes 786436
  1014.7 92.2 %all-reduce.20.cloned.1.call-start = ((), (), s32[]{:S(2)}) async-start(), calls=%async_computation.2 | async-start | bytes 1048576 | tf_op jit(solution)/shard_map/psum | solution.py:12
  1065.3 2.0 copy-start.9
  1068.2 106.5 %all-reduce.22.cloned.1.call-start = ((), (), s32[]{:S(2)}) async-start(), calls=%async_computation.3 | async-start | bytes 524288 | tf_op jit(solution)/shard_map/psum | solution.py:67
  1106.9 10.1 copy-start.10
  1128.0 3.4 copy-start
  1131.4 1.9 copy-start.3
  1137.6 470.9 %all-reduce.24.cloned.1.call-start = ((), (), s32[]{:S(2)}) async-start(), calls=%async_computation.4 | async-start | bytes 8388608 | tf_op jit(solution)/shard_map/psum | solution.py:12
  1237.3 3.7 copy-start.4
  1245.0 1.4 copy-start.14
  1248.9 422.5 %all-reduce.32.cloned.1.call-start = ((), (), s32[]{:S(2)}) async-start(), calls=%async_computation.10 | async-start | bytes 1572864 | tf_op jit(solution)/shard_map/psum | solution.py:12
  1610.4 506.9 %all-reduce.28.cloned.1.call-start = ((), (), s32[]{:S(2)}) async-start(), calls=%async_computation.8 | async-start | bytes 8912896 | tf_op jit(solution)/shard_map/psum | solution.py:79
  1671.4 65.6 %copy-start.15 = (f32[512,256]{0,1:T(8,128)S(1)}, f32[512,256]{0,1:T(8,128)}, u32[]{:S(2)}) copy-start(f32[512,256]{0,1:T(8,128)} %get-tuple-element.93) | copy-start | bytes 1572868
  1754.6 415.3 %all-gather.7.cloned.1.call-start = ((), (), s32[]{:S(2)}) async-start(), calls=%async_computation.7 | async-start | bytes 1310720 | tf_op jit(solution)/shard_map/all_gather | solution.py:81
  2117.3 7.4 copy-start.6
  2122.8 2.0 copy-start.8
  2129.1 42.2 %copy-start.17 = (f32[256,256]{0,1:T(8,128)S(1)}, f32[256,256]{0,1:T(8,128)}, u32[]{:S(2)}) copy-start(f32[256,256]{0,1:T(8,128)} %get-tuple-element.90) | copy-start | bytes 786436
  2129.1 92.2 %all-reduce.26.cloned.1.call-start = ((), (), s32[]{:S(2)}) async-start(), calls=%async_computation.5 | async-start | bytes 1048576 | tf_op jit(solution)/shard_map/psum | solution.py:12
  2179.7 2.0 copy-start.11
  2221.3 9.6 copy-start.12
Sparse Core Ops, SparseCore 0:
  24.3 39.6 all-reduce.15
  137.8 359.3 all-reduce.17
  499.9 60.0 all-reduce.33
  637.1 362.3 all-reduce.29
  1014.8 40.7 all-gather.4
  1068.3 38.5 all-reduce.19
  1137.7 36.9 all-reduce.21
  1249.0 359.3 all-reduce.23
  1611.2 60.1 all-reduce.31
  1754.8 362.5 all-reduce.27
  2129.2 40.7 all-gather.6
  2182.7 38.4 all-reduce.25
